TPU v7x, 32 devices: a whole 2x2x4 slice. The times are simulated.
32 devices in a mesh: tm: 8 (over y, x, core), sector: 4 (over z).
Axes of the slice: x: 2, y: 2, z: 4, core: 2. Of those that a mesh axis runs over, the one named last changes fastest.
Arguments:
- propagator: bfloat16 [4, 8, 640, 640], P('sector', 'tm'), may hold values from -6 to 6
- rising_op: bfloat16 [4, 640, 640], P('sector'), may hold values from -0.25 to 0.25
- energies: float32 [4, 640], P('sector'), may hold values from 0.5 to 40
- hyb_particle: float32 [8], P('tm'), may hold values from 0.2 to 1
- hyb_hole: float32 [8], P('tm'), may hold values from 0.2 to 1
- sector_sizes: int32 [4], P('sector'), may hold values from 160 to 640, as said below
Outputs:
- new_prop: bfloat16 [4, 8, 640, 640], P('sector', 'tm')
Inputs may be any that keep to these rules, and one draw needn't show every extreme that they name: `sector_sizes`: one sector holds exactly 640 states.
All inputs are finite; a program needn't handle non-finite values.
Results may differ from a plain program's by a relative error of at most 0.0061.
Values may be sent and summed in bfloat16 or wider, within the bound.
A program may use at most 128 MiB of HBM per device.

v0:
```python
import jax
import jax.numpy as jnp
from jax import lax
from jax.sharding import PartitionSpec as P


def shifted(block, axis, distance):
    devices = range(lax.axis_size(axis))
    route = [(i - distance, i) for i in devices if i - distance in devices]
    return lax.ppermute(block, axis, route)


def per_device(propagator, rising_op, energies, hyb_particle, hyb_hole, sector_sizes):
    t_dev = propagator.shape[1]
    states = propagator.shape[2]
    time_count = t_dev * lax.axis_size("tm")
    step_size = 1.0 / time_count
    positions = jnp.arange(states, dtype=jnp.int32)
    live_mask = positions < sector_sizes[0]
    square = live_mask[:, None] & live_mask[None, :]
    masked_prop = jnp.where(square[None], propagator[0], jnp.zeros((), jnp.bfloat16))
    operator = rising_op[0]
    raised = jnp.einsum(
        "ik,tkl->til", operator, masked_prop, preferred_element_type=jnp.float32
    ).astype(jnp.bfloat16)
    upward = jnp.einsum("tik,jk->tij", raised, operator, preferred_element_type=jnp.float32).astype(
        jnp.bfloat16
    )
    from_below = shifted(upward, "sector", 1)
    from_above = shifted(masked_prop, "sector", -1)
    lowered = jnp.einsum(
        "ki,tkl->til", operator, from_above, preferred_element_type=jnp.float32
    ).astype(jnp.bfloat16)
    downward = jnp.einsum("tik,kl->til", lowered, operator, preferred_element_type=jnp.float32)
    combined = (
        hyb_particle[:, None, None] * from_below.astype(jnp.float32)
        + hyb_hole[:, None, None] * downward
    )
    self_energy = jnp.where(square[None], combined, jnp.zeros((), jnp.float32)).astype(jnp.bfloat16)
    rows_each = states // lax.axis_size("tm")
    first_row = lax.axis_index("tm") * rows_each
    lag_rows = lax.all_to_all(self_energy, "tm", split_axis=1, concat_axis=0, tiled=True)
    history = lax.all_gather(masked_prop, "tm", axis=0, tiled=True)
    mirrored = jnp.concatenate([history[::-1], history], 0)
    slots = jnp.arange(time_count, dtype=jnp.int32)
    wide_slots = jnp.arange(time_count + 1, dtype=jnp.int32)

    def pair_step(lag, sums):
        forward, backward = sums
        other = time_count - 1 - lag
        window = lax.dynamic_slice_in_dim(mirrored, lag, time_count + 1, 0)
        near = lax.dynamic_index_in_dim(lag_rows, lag, 0, keepdims=False)
        far = lax.dynamic_index_in_dim(lag_rows, other, 0, keepdims=False)
        left = jnp.where((wide_slots < time_count - lag)[:, None, None], near[None], far[None])
        product = jnp.einsum("uik,ukl->uil", left, window, preferred_element_type=jnp.float32)
        backward = backward + jnp.where(
            (slots < time_count - lag)[:, None, None],
            product[:time_count],
            jnp.zeros((), jnp.float32),
        )
        forward = forward + jnp.where(
            (slots >= time_count - lag - 1)[:, None, None], product[1:], jnp.zeros((), jnp.float32)
        )
        return (forward, backward)

    empty_rows = jnp.zeros((time_count, rows_each, states), jnp.float32)
    forward, backward = lax.fori_loop(0, time_count // 2, pair_step, (empty_rows, empty_rows))
    convolved = step_size * (forward + backward[::-1])
    row_ids = first_row + jnp.arange(rows_each, dtype=jnp.int32)
    row_rates = lax.dynamic_slice_in_dim(energies[0], first_row, rows_each, 0)
    decay_rows = jnp.exp(-step_size * row_rates)

    def advance(running, term):
        running = decay_rows[:, None] * running + term
        return (running, running)

    _, summed = lax.scan(advance, jnp.zeros((rows_each, states), jnp.float32), convolved)
    moments = jnp.arange(time_count).astype(jnp.float32) * step_size
    live_rows = row_ids < sector_sizes[0]
    free_part = jnp.where(
        live_rows[None, :],
        jnp.exp(-row_rates[None, :] * moments[:, None]),
        jnp.zeros((), jnp.float32),
    )
    diagonal = jnp.where(
        (row_ids[:, None] == positions[None, :])[None],
        free_part[:, :, None],
        jnp.zeros((), jnp.float32),
    )
    new_rows = (diagonal - step_size * summed).astype(jnp.bfloat16)
    return lax.all_to_all(new_rows, "tm", split_axis=0, concat_axis=1, tiled=True)[None]


def solution(mesh):
    placed = (
        P("sector", "tm", None, None),
        P("sector", None, None),
        P("sector", None),
        P("tm"),
        P("tm"),
        P("sector"),
    )
    return jax.shard_map(
        per_device,
        mesh=mesh,
        in_specs=placed,
        out_specs=P("sector", "tm", None, None),
        check_vma=False,
    )
```

profile of v0, /device:TPU:0, one launch (start us, length us, event | category | flops | bytes accessed | tf_op | source)
XLA Modules:
  0.0 162.4 jit_solution(225361923420501898)
XLA Ops:
  7.3 2.4 %and_select_fusion.1 = bf16[1,640,640]{2,1,0:T(8,128)(2,1)} fusion(bf16[1,1,640,640]{3,2,1,0:T(8,128)(2,1)} %param.10, pred[640]{0:T(1024)(128)(4,1)S(1)} %iota_compare_fusion.4), kind=kLoop, calls=%fused_computation.23 | loop fusion | flops 819200 | bytes 1639040 | tf_op jit(solution)/shard_map/jit(_where)/select_n | solution.py:21
  9.7 0.0 all-gather.2.cloned.1.call-update
  9.7 1.3 collective-permute-start.1
  11.0 2.9 %fusion.15 = bf16[1,640,640]{2,1,0:T(8,128)(2,1)} fusion(bf16[1,1,640,640]{3,2,1,0:T(8,128)(2,1)S(1)} %copy-done.1, bf16[1,640,640]{2,1,0:T(8,128)(2,1)S(1)} %copy-done, pred[640]{0:T(1024)(128)(4,1)S(1)} %iota_compare_fusion.4), kind=kOutput, calls=%fused_computation.33 | convolution fusion | flops 1050214400 | bytes 2458240 | tf_op jit(solution)/shard_map/tik,jk->tij/dot_general | solution.py:26
  13.9 5.6 %collective-permute-start = (bf16[1,640,640]{2,1,0:T(8,128)(2,1)}, bf16[1,640,640]{2,1,0:T(8,128)(2,1)S(1)}, u32[]{:S(2)}, u32[]{:S(2)}) collective-permute-start(bf16[1,640,640]{2,1,0:T(8,128)(2,1)} %fusion.15), channel_id=1, source_target_pairs={{0,1},{1,2},{2,3},{4,5},{5,6},{6,7},{8,9},{9,10},{10,11},{12,13},{... | collective-permute-start | bytes 2457608 | tf_op jit(solution)/shard_map/ppermute | solution.py:10
  20.9 12.3 %collective-permute-done.1 = bf16[1,640,640]{2,1,0:T(8,128)(2,1)S(1)} collective-permute-done((bf16[1,640,640]{2,1,0:T(8,128)(2,1)}, bf16[1,640,640]{2,1,0:T(8,128)(2,1)S(1)}, u32[]{:S(2)}, u32[]{:S(2)}) %collective-permute-start.1) | collective-permute-done | bytes 819232 | tf_op jit(solution)/shard_map/ppermute | solution.py:10
  33.1 4.2 %collective-permute-done = bf16[1,640,640]{2,1,0:T(8,128)(2,1)S(1)} collective-permute-done((bf16[1,640,640]{2,1,0:T(8,128)(2,1)}, bf16[1,640,640]{2,1,0:T(8,128)(2,1)S(1)}, u32[]{:S(2)}, u32[]{:S(2)}) %collective-permute-start) | collective-permute-done | bytes 819232 | tf_op jit(solution)/shard_map/ppermute | solution.py:10
  37.3 3.7 %fusion.13 = bf16[1,640,640]{2,1,0:T(8,128)(2,1)S(1)} fusion(bf16[1,640,640]{2,1,0:T(8,128)(2,1)S(1)} %collective-permute-done, bf16[1,640,640]{2,1,0:T(8,128)(2,1)} %copy-done.2, bf16[1,640,640]{2,1,0:T(8,128)(2,1)S(1)} %copy-done, f32[]{:T(128)} %bitcast.66, f32[]{:T(128)} %bitcast.65, pred[640]{0:T(1024)(128)(4,1)S(1)} %iota_compare_fusion.4), kind=kOutput, calls=%fused_computation.24 | convolution fusion | flops 1051852800 | bytes 3277448 | tf_op jit(solution)/shard_map/tik,kl->til/dot_general | solution.py:34
  41.0 1.3 copy.11
  42.3 0.5 broadcast.254
  42.8 5.6 %reduce = bf16[640,640]{1,0:T(8,128)(2,1)S(1)} reduce(bf16[640,1,640]{2,1,0:T(2,128)(2,1)S(1)} %bitcast.69, bf16[]{:T(256)} %broadcast.254), dimensions={1}, to_apply=%bitcast.60.reduce_sub_computation | reduce | bytes 1638402
  48.4 1.1 reshape.286
  49.5 4.4 %all-to-all-start = ((bf16[8,2,25600]{2,1,0:T(2,128)(2,1)}), bf16[8,2,25600]{2,1,0:T(2,128)(2,1)}, u32[]{:S(2)}, u32[]{:S(2)}) async-start(bf16[8,2,25600]{2,1,0:T(2,128)(2,1)} %reshape.286), calls=%async_computation | async-start | bytes 1638400 | tf_op jit(solution)/shard_map/all_to_all | solution.py:42
  54.0 0.8 negate_bitcast_fusion
  54.8 0.1 exponential_select_fusion
  54.8 0.1 iota_compare_fusion.3
  54.9 12.1 %all-to-all-done = bf16[8,2,25600]{2,1,0:T(2,128)(2,1)} async-done(((bf16[8,2,25600]{2,1,0:T(2,128)(2,1)}), bf16[8,2,25600]{2,1,0:T(2,128)(2,1)}, u32[]{:S(2)}, u32[]{:S(2)}) %all-to-all-start) | async-done | bytes 819232 | tf_op jit(solution)/shard_map/all_to_all | solution.py:42
  67.1 4.0 %reshape.287 = bf16[640,1,640]{2,1,0:T(2,128)(2,1)S(1)} reshape(bf16[8,2,25600]{2,1,0:T(2,128)(2,1)} %all-to-all-done) | data formatting | bytes 1638400
  71.1 1.0 copy.9
  72.1 6.3 %rev.6 = bf16[8,640,640]{2,1,0:T(8,128)(2,1)} reverse(bf16[8,640,640]{2,1,0:T(8,128)(2,1)} %all-gather.2.cloned.1.call-done), dimensions={0} | reverse | bytes 13107200 | tf_op jit(solution)/shard_map/rev | solution.py:44
  78.5 12.3 %pad_maximum_fusion = bf16[16,640,640]{2,1,0:T(8,128)(2,1)} fusion(bf16[8,640,640]{2,1,0:T(8,128)(2,1)} %all-gather.2.cloned.1.call-done, bf16[8,640,640]{2,1,0:T(8,128)(2,1)} %rev.6), kind=kLoop, calls=%fused_computation.21 | loop fusion | flops 6553600 | bytes 26214400 | tf_op jit(solution)/shard_map/concatenate | solution.py:44
  90.8 36.5 %while.35 = (s32[]{:T(128)}, f32[8,80,640]{2,1,0:T(8,128)}, f32[8,80,640]{2,1,0:T(8,128)}, bf16[8,80,640]{2,1,0:T(8,128)(2,1)}, bf16[16,640,640]{2,1,0:T(8,128)(...) while((s32[]{:T(128)}, f32[8,80,640]{2,1,0:T(8,128)}, ...), condition=%wide.region_1.2_spmd.clone.clone, body=%wide.region_0.1_spmd.clone.clone.sunk | while | flops 592742400 | bytes 19661552 | solution.py:67
  90.8 1.0 dynamic-slice_bitcast_fusion.3
  91.8 4.6 %fusion.40 = f32[9,80,640]{2,1,0:T(8,128)S(1)} fusion(bf16[16,640,640]{2,1,0:T(8,128)(2,1)} %get-tuple-element.458, s32[]{:T(128)} %get-tuple-element.444, pred[9]{0:T(512)(128)(4,1)S(1)} %iota_compare_fusion.7, bf16[80,640]{1,0:T(8,128)(2,1)S(1)} %get-tuple-element.428, bf16[80,640]{1,0:T(8,128)(2,1)S(1)} %get-tuple-element.429), kind=kOutput, calls=%fused_computation.5.clone.1 | convolution fusion | flops 590284800 | bytes 9421321 | tf_op jit(solution)/shard_map/while/body/eval_jaxpr/uik,ukl->uil/dot_general | solution.py:55
  96.4 2.1 %fusion.41 = (f32[8,80,640]{2,1,0:T(8,128)}, f32[8,80,640]{2,1,0:T(8,128)}) fusion(f32[9,80,640]{2,1,0:T(8,128)S(1)} %fusion.40, f32[8,80,640]{2,1,0:T(8,128)} %get-tuple-element.446, pred[8]{0:T(512)(128)(4,1)S(1)} %get-tuple-element.430, pred[]{:T(512)S(6)} %compare.7, pred[8]{0:T(512)(128)(4,1)S(1)} %get-tuple-element.431, ...), kind=kLoop, calls=%fused_computation.8.clone.1 | loop fusion | flops 2457600 | bytes 9830417 | tf_op jit(solution)/shard_map/while/body/eval_jaxpr/add | solution.py:56
  98.5 1.0 dynamic-slice_bitcast_fusion.3
  99.5 4.6 %fusion.40 = f32[9,80,640]{2,1,0:T(8,128)S(1)} fusion(bf16[16,640,640]{2,1,0:T(8,128)(2,1)} %get-tuple-element.458, s32[]{:T(128)} %get-tuple-element.444, pred[9]{0:T(512)(128)(4,1)S(1)} %iota_compare_fusion.7, bf16[80,640]{1,0:T(8,128)(2,1)S(1)} %get-tuple-element.428, bf16[80,640]{1,0:T(8,128)(2,1)S(1)} %get-tuple-element.429), kind=kOutput, calls=%fused_computation.5.clone.1 | convolution fusion | flops 590284800 | bytes 9421321 | tf_op jit(solution)/shard_map/while/body/eval_jaxpr/uik,ukl->uil/dot_general | solution.py:55
  104.1 4.0 %fusion.41 = (f32[8,80,640]{2,1,0:T(8,128)}, f32[8,80,640]{2,1,0:T(8,128)}) fusion(f32[9,80,640]{2,1,0:T(8,128)S(1)} %fusion.40, f32[8,80,640]{2,1,0:T(8,128)} %get-tuple-element.446, pred[8]{0:T(512)(128)(4,1)S(1)} %get-tuple-element.430, pred[]{:T(512)S(6)} %compare.7, pred[8]{0:T(512)(128)(4,1)S(1)} %get-tuple-element.431, ...), kind=kLoop, calls=%fused_computation.8.clone.1 | loop fusion | flops 2457600 | bytes 9830417 | tf_op jit(solution)/shard_map/while/body/eval_jaxpr/add | solution.py:56
  108.1 1.0 dynamic-slice_bitcast_fusion.3
  109.1 4.6 %fusion.40 = f32[9,80,640]{2,1,0:T(8,128)S(1)} fusion(bf16[16,640,640]{2,1,0:T(8,128)(2,1)} %get-tuple-element.458, s32[]{:T(128)} %get-tuple-element.444, pred[9]{0:T(512)(128)(4,1)S(1)} %iota_compare_fusion.7, bf16[80,640]{1,0:T(8,128)(2,1)S(1)} %get-tuple-element.428, bf16[80,640]{1,0:T(8,128)(2,1)S(1)} %get-tuple-element.429), kind=kOutput, calls=%fused_computation.5.clone.1 | convolution fusion | flops 590284800 | bytes 9421321 | tf_op jit(solution)/shard_map/while/body/eval_jaxpr/uik,ukl->uil/dot_general | solution.py:55
  113.7 4.0 %fusion.41 = (f32[8,80,640]{2,1,0:T(8,128)}, f32[8,80,640]{2,1,0:T(8,128)}) fusion(f32[9,80,640]{2,1,0:T(8,128)S(1)} %fusion.40, f32[8,80,640]{2,1,0:T(8,128)} %get-tuple-element.446, pred[8]{0:T(512)(128)(4,1)S(1)} %get-tuple-element.430, pred[]{:T(512)S(6)} %compare.7, pred[8]{0:T(512)(128)(4,1)S(1)} %get-tuple-element.431, ...), kind=kLoop, calls=%fused_computation.8.clone.1 | loop fusion | flops 2457600 | bytes 9830417 | tf_op jit(solution)/shard_map/while/body/eval_jaxpr/add | solution.py:56
  117.7 1.0 dynamic-slice_bitcast_fusion.3
  118.7 4.6 %fusion.40 = f32[9,80,640]{2,1,0:T(8,128)S(1)} fusion(bf16[16,640,640]{2,1,0:T(8,128)(2,1)} %get-tuple-element.458, s32[]{:T(128)} %get-tuple-element.444, pred[9]{0:T(512)(128)(4,1)S(1)} %iota_compare_fusion.7, bf16[80,640]{1,0:T(8,128)(2,1)S(1)} %get-tuple-element.428, bf16[80,640]{1,0:T(8,128)(2,1)S(1)} %get-tuple-element.429), kind=kOutput, calls=%fused_computation.5.clone.1 | convolution fusion | flops 590284800 | bytes 9421321 | tf_op jit(solution)/shard_map/while/body/eval_jaxpr/uik,ukl->uil/dot_general | solution.py:55
  123.3 4.0 %fusion.41 = (f32[8,80,640]{2,1,0:T(8,128)}, f32[8,80,640]{2,1,0:T(8,128)}) fusion(f32[9,80,640]{2,1,0:T(8,128)S(1)} %fusion.40, f32[8,80,640]{2,1,0:T(8,128)} %get-tuple-element.446, pred[8]{0:T(512)(128)(4,1)S(1)} %get-tuple-element.430, pred[]{:T(512)S(6)} %compare.7, pred[8]{0:T(512)(128)(4,1)S(1)} %get-tuple-element.431, ...), kind=kLoop, calls=%fused_computation.8.clone.1 | loop fusion | flops 2457600 | bytes 9830417 | tf_op jit(solution)/shard_map/while/body/eval_jaxpr/add | solution.py:56
  127.3 3.3 %add_multiply_fusion = f32[8,80,640]{2,1,0:T(8,128)} fusion(f32[8,80,640]{2,1,0:T(8,128)} %get-tuple-element.265, f32[8,80,640]{2,1,0:T(8,128)} %get-tuple-element.266), kind=kLoop, calls=%fused_computation.27 | loop fusion | flops 819200 | bytes 4915200 | tf_op jit(solution)/shard_map/mul | solution.py:68
  130.6 0.1 broadcast_in_dim.232
  130.7 8.4 %while.34 = (s32[]{:T(128)}, f32[80,640]{1,0:T(8,128)S(1)}, f32[8,80,640]{2,1,0:T(8,128)S(1)}, f32[80]{0:T(128)S(1)}, f32[8,80,640]{2,1,0:T(8,128)}, /*index=5*/s32[]{:T(128)}, s32[]{:T(128)}) while((s32[]{:T(128)}, f32[80,640]{1,0:T(8,128)S(1)}, f32[8,80,640]{2,1,0:T(8,128)S(1)}, f32[80]{0:T(128)S(1)}, f32[8,80,640]{2,1,0:T(8,128)}, ...), condition=%wide.region_3.4_spmd.clone, body=%wide.region_2.3_spmd.clone.sunk | while | flops 153603 | bytes 819803 | solution.py:77
  130.7 1.0 bitcast_dynamic-update-slice_fusion.2
  131.7 1.0 bitcast_dynamic-update-slice_fusion.2
  132.8 1.0 bitcast_dynamic-update-slice_fusion.2
  133.8 1.0 bitcast_dynamic-update-slice_fusion.2
  134.9 1.0 bitcast_dynamic-update-slice_fusion.2
  135.9 1.0 bitcast_dynamic-update-slice_fusion.2
  137.0 1.0 bitcast_dynamic-update-slice_fusion.2
  138.0 1.0 bitcast_dynamic-update-slice_fusion.2
  139.1 0.3 subtract_convert_fusion
  139.4 15.3 %all_to_all.21 = bf16[8,80,640]{2,1,0:T(8,128)(2,1)S(1)} all-to-all(bf16[8,80,640]{2,1,0:T(8,128)(2,1)S(1)} %subtract_convert_fusion), channel_id=1, replica_groups=mesh['tm'=8,'sector'=4] {'tm'}, dimensions={0} | all-to-all | bytes 1638400 | tf_op jit(solution)/shard_map/all_to_all | solution.py:91
  154.6 0.9 copy.35
  (23 shorter events, 0.1 us)
Async XLA Ops:
  6.5 4.5 %copy-start = (bf16[1,640,640]{2,1,0:T(8,128)(2,1)S(1)}, bf16[1,640,640]{2,1,0:T(8,128)(2,1)}, u32[]{:S(2)}) copy-start(bf16[1,640,640]{2,1,0:T(8,128)(2,1)} %param.11) | copy-start | bytes 2457604
  6.5 4.5 %copy-start.1 = (bf16[1,1,640,640]{3,2,1,0:T(8,128)(2,1)S(1)}, bf16[1,1,640,640]{3,2,1,0:T(8,128)(2,1)}, u32[]{:S(2)}) copy-start(bf16[1,1,640,640]{3,2,1,0:T(8,128)(2,1)} %param.10) | copy-start | bytes 2457604
  6.5 65.6 %all-gather.2.cloned.1.call-start = ((), (), s32[]{:S(2)}) async-start(), calls=%async_computation.2 | async-start | bytes 7372800 | tf_op jit(solution)/shard_map/all_gather | solution.py:43
  9.7 23.4 %collective-permute-start.1 = (bf16[1,640,640]{2,1,0:T(8,128)(2,1)}, bf16[1,640,640]{2,1,0:T(8,128)(2,1)S(1)}, u32[]{:S(2)}, u32[]{:S(2)}) collective-permute-start(bf16[1,640,640]{2,1,0:T(8,128)(2,1)} %and_select_fusion.1), channel_id=1, source_target_pairs={{1,0},{2,1},{3,2},{5,4},{6,5},{7,6},{9,8},{10,9},{11,10},{13,12},{... | collective-permute-start | bytes 2457608 | tf_op jit(solution)/shard_map/ppermute | solution.py:10
  13.9 23.4 %collective-permute-start = (bf16[1,640,640]{2,1,0:T(8,128)(2,1)}, bf16[1,640,640]{2,1,0:T(8,128)(2,1)S(1)}, u32[]{:S(2)}, u32[]{:S(2)}) collective-permute-start(bf16[1,640,640]{2,1,0:T(8,128)(2,1)} %fusion.15), channel_id=1, source_target_pairs={{0,1},{1,2},{2,3},{4,5},{5,6},{6,7},{8,9},{9,10},{10,11},{12,13},{... | collective-permute-start | bytes 2457608 | tf_op jit(solution)/shard_map/ppermute | solution.py:10
  33.1 4.2 %copy-start.2 = (bf16[1,640,640]{2,1,0:T(8,128)(2,1)}, bf16[1,640,640]{2,1,0:T(8,128)(2,1)S(1)}, u32[]{:S(2)}) copy-start(bf16[1,640,640]{2,1,0:T(8,128)(2,1)S(1)} %collective-permute-done.1) | copy-start | bytes 2457604
  49.5 17.6 %all-to-all-start = ((bf16[8,2,25600]{2,1,0:T(2,128)(2,1)}), bf16[8,2,25600]{2,1,0:T(2,128)(2,1)}, u32[]{:S(2)}, u32[]{:S(2)}) async-start(bf16[8,2,25600]{2,1,0:T(2,128)(2,1)} %reshape.286), calls=%async_computation | async-start | bytes 1638400 | tf_op jit(solution)/shard_map/all_to_all | solution.py:42
Sparse Core Ops, SparseCore 0:
  9.8 49.5 all-gather.1
where the time goes:
time: 164 us; the launch traced here: 162 us
  other arithmetic  47.3 us (29%)
  waiting for transfers between devices  28.6 us (17%)
  matrix products  24.9 us (15%)
  local copies, waits for them, and re-layouts  19.1 us (12%)
  between operations  15.6 us (10%)
  blocking collectives  15.3 us (9%)
  starting transfers between devices  11.3 us (7%)
    dot_general x4, matrix products, pair_step(): jnp.einsum('uik,ukl->uil', left, window, preferred_element_type=jnp.float32)  18.3 us
    ppermute x2, waiting for transfers between devices, shifted(): return lax.ppermute(block, axis, route)  16.4 us
    all_to_all x1, blocking collectives, per_device(): lax.all_to_all(new_rows, 'tm', split_axis=0, concat_axis=1, tiled=True)  15.3 us
    add x4, other arithmetic, pair_step(): backward + jnp.where((slots < time_count - lag)[:, None, None], product[:...  14.2 us
    concatenate x1, other arithmetic, per_device(): mirrored = jnp.concatenate([history[::-1], history], 0)  12.3 us
    all_to_all x1, waiting for transfers between devices, per_device(): lax.all_to_all(self_energy, 'tm', split_axis=1, concat_axis=0, tiled=True)  12.1 us
    dynamic_update_slice x8, other arithmetic, per_device(): lax.scan(advance, jnp.zeros((rows_each, states), jnp.float32), convolved)  8.25 us
    unnamed x11, local copies, waits for them, and re-layouts  7.55 us
  transfers between devices with their start and end apart: 4, of which 3 were waited for; matrix products, arithmetic and copies ran while one was open for 13% of the time, Pallas kernels for 0%

commit v1 on v0

--- a/solution.py
+++ b/solution.py
@@ -2,6 +2,18 @@
 import jax.numpy as jnp
 from jax import lax
 from jax.sharding import PartitionSpec as P
+
+
+def trails_compute(mat):
+    return jnp.concatenate(
+        jax.lax.all_to_all(
+            jnp.stack(jnp.split(mat, jax.lax.axis_size("tm"), axis=1), axis=0),
+            axis_name="tm",
+            split_axis=0,
+            concat_axis=0,
+        ),
+        axis=0,
+    )
 
 
 def shifted(block, axis, distance):
@@ -39,7 +51,7 @@
     self_energy = jnp.where(square[None], combined, jnp.zeros((), jnp.float32)).astype(jnp.bfloat16)
     rows_each = states // lax.axis_size("tm")
     first_row = lax.axis_index("tm") * rows_each
-    lag_rows = lax.all_to_all(self_energy, "tm", split_axis=1, concat_axis=0, tiled=True)
+    lag_rows = trails_compute(self_energy)
     history = lax.all_gather(masked_prop, "tm", axis=0, tiled=True)
     mirrored = jnp.concatenate([history[::-1], history], 0)
     slots = jnp.arange(time_count, dtype=jnp.int32)

time: 164 us -> 158 us (0.963)
  other arithmetic: 47.3 us -> 41.7 us
  blocking collectives: 15.3 us -> 19.1 us
  local copies, waits for them, and re-layouts: 19.1 us -> 17.3 us
    all_to_all x1, waiting for transfers between devices: 12.1 us -> 0.01 us  [trails_compute(): jax.lax.all_to_all(jnp.stack(jnp.split(mat, jax.lax.axis_size('tm'), axis...]
    all_gather x1, waiting for transfers between devices: 0.01 us -> 11.9 us  [per_device(): history = lax.all_gather(masked_prop, 'tm', axis=0, tiled=True)]
    unnamed x4 -> x3, other arithmetic: 5.64 us -> 0.01 us
    all_to_all x1, blocking collectives: 15.3 us -> 19.1 us  [per_device(): lax.all_to_all(new_rows, 'tm', split_axis=0, concat_axis=1, tiled=True)]
    unnamed x11 -> x14, local copies, waits for them, and re-layouts: 7.55 us -> 6.34 us
  transfers between devices with their start and end apart: 4 -> 4, of which waited for: 3 -> 3; matrix products, arithmetic and copies ran while one was open for 13% -> 20% of each run, Pallas kernels for 0% -> 0%
where the time goes in v1:
time: 158 us; the launch traced here: 157 us
  other arithmetic  41.7 us (26%)
  waiting for transfers between devices  27.3 us (17%)
  matrix products  24.6 us (16%)
  blocking collectives  19.1 us (12%)
  local copies, waits for them, and re-layouts  17.3 us (11%)
  between operations  15.6 us (10%)
  starting transfers between devices  11.1 us (7%)
    all_to_all x1, blocking collectives, per_device(): lax.all_to_all(new_rows, 'tm', split_axis=0, concat_axis=1, tiled=True)  19.1 us
    dot_general x4, matrix products, pair_step(): jnp.einsum('uik,ukl->uil', left, window, preferred_element_type=jnp.float32)  18.3 us
    ppermute x2, waiting for transfers between devices, shifted(): return lax.ppermute(block, axis, route)  15.4 us
    add x4, other arithmetic, pair_step(): backward + jnp.where((slots < time_count - lag)[:, None, None], product[:...  14.1 us
    concatenate x1, other arithmetic, per_device(): mirrored = jnp.concatenate([history[::-1], history], 0)  12.4 us
    all_gather x1, waiting for transfers between devices, per_device(): history = lax.all_gather(masked_prop, 'tm', axis=0, tiled=True)  11.9 us
    dynamic_update_slice x8, other arithmetic, per_device(): lax.scan(advance, jnp.zeros((rows_each, states), jnp.float32), convolved)  8.25 us
    ppermute x2, starting transfers between devices, shifted(): return lax.ppermute(block, axis, route)  6.92 us
  transfers between devices with their start and end apart: 4, of which 3 were waited for; matrix products, arithmetic and copies ran while one was open for 20% of the time, Pallas kernels for 0%

profile of v1, /device:TPU:0, one launch (start us, length us, event | category | flops | bytes accessed | tf_op | source)
XLA Modules:
  0.0 157.0 jit_solution(1185447009855135495)
XLA Ops:
  7.3 2.3 %and_select_fusion.1 = bf16[1,640,640]{2,1,0:T(8,128)(2,1)} fusion(bf16[1,1,640,640]{3,2,1,0:T(8,128)(2,1)} %param.10, pred[640]{0:T(1024)(128)(4,1)S(1)} %iota_compare_fusion.4), kind=kLoop, calls=%fused_computation.23 | loop fusion | flops 819200 | bytes 1639040 | tf_op jit(solution)/shard_map/jit(_where)/select_n | solution.py:33
  9.7 1.3 collective-permute-start.1
  11.0 2.9 %fusion.15 = bf16[1,640,640]{2,1,0:T(8,128)(2,1)} fusion(bf16[1,1,640,640]{3,2,1,0:T(8,128)(2,1)S(1)} %copy-done.1, bf16[1,640,640]{2,1,0:T(8,128)(2,1)S(1)} %copy-done, pred[640]{0:T(1024)(128)(4,1)S(1)} %iota_compare_fusion.4), kind=kOutput, calls=%fused_computation.33 | convolution fusion | flops 1050214400 | bytes 2458240 | tf_op jit(solution)/shard_map/tik,jk->tij/dot_general | solution.py:38
  13.9 5.6 %collective-permute-start = (bf16[1,640,640]{2,1,0:T(8,128)(2,1)}, bf16[1,640,640]{2,1,0:T(8,128)(2,1)S(1)}, u32[]{:S(2)}, u32[]{:S(2)}) collective-permute-start(bf16[1,640,640]{2,1,0:T(8,128)(2,1)} %fusion.15), channel_id=1, source_target_pairs={{0,1},{1,2},{2,3},{4,5},{5,6},{6,7},{8,9},{9,10},{10,11},{12,13},{... | collective-permute-start | bytes 2457608 | tf_op jit(solution)/shard_map/ppermute | solution.py:22
  20.9 0.8 negate_bitcast_fusion
  21.9 11.2 %collective-permute-done.1 = bf16[1,640,640]{2,1,0:T(8,128)(2,1)S(1)} collective-permute-done((bf16[1,640,640]{2,1,0:T(8,128)(2,1)}, bf16[1,640,640]{2,1,0:T(8,128)(2,1)S(1)}, u32[]{:S(2)}, u32[]{:S(2)}) %collective-permute-start.1) | collective-permute-done | bytes 819232 | tf_op jit(solution)/shard_map/ppermute | solution.py:22
  33.1 4.2 %collective-permute-done = bf16[1,640,640]{2,1,0:T(8,128)(2,1)S(1)} collective-permute-done((bf16[1,640,640]{2,1,0:T(8,128)(2,1)}, bf16[1,640,640]{2,1,0:T(8,128)(2,1)S(1)}, u32[]{:S(2)}, u32[]{:S(2)}) %collective-permute-start) | collective-permute-done | bytes 819232 | tf_op jit(solution)/shard_map/ppermute | solution.py:22
  37.3 0.9 copy-done.2
  38.2 3.5 %fusion.13 = bf16[1,640,640]{2,1,0:T(8,128)(2,1)S(1)} fusion(bf16[1,640,640]{2,1,0:T(8,128)(2,1)} %copy-done.2, bf16[1,640,640]{2,1,0:T(8,128)(2,1)S(1)} %collective-permute-done.1, bf16[1,640,640]{2,1,0:T(8,128)(2,1)S(1)} %copy-done, f32[]{:T(128)} %bitcast.94, f32[]{:T(128)} %bitcast.93, pred[640]{0:T(1024)(128)(4,1)S(1)} %iota_compare_fusion.4), kind=kOutput, calls=%fused_computation.24 | convolution fusion | flops 1051852800 | bytes 3277448 | tf_op jit(solution)/shard_map/tik,kl->til/dot_general | solution.py:46
  41.7 0.7 fusion.39
  42.3 0.7 fusion.38
  43.0 0.7 fusion.37
  43.6 0.7 fusion.36
  44.3 0.7 fusion.35
  44.9 0.7 fusion.34
  45.6 0.7 fusion.33
  46.2 0.7 fusion.32
  46.9 4.2 %all-to-all-start = ((bf16[8,1,80,640]{3,2,1,0:T(8,128)(2,1)}), bf16[8,1,80,640]{3,2,1,0:T(8,128)(2,1)}, u32[]{:S(2)}, u32[]{:S(2)}) async-start(bf16[8,1,80,640]{3,2,1,0:T(8,128)(2,1)} %fusion.32), calls=%async_computation | async-start | bytes 1638400 | tf_op jit(solution)/shard_map/all_to_all | solution.py:9
  51.1 11.9 %all-gather.2.cloned.1.call-done = bf16[8,640,640]{2,1,0:T(8,128)(2,1)} async-done(((bf16[1,640,640]{2,1,0:T(8,128)(2,1)}), bf16[8,640,640]{2,1,0:T(8,128)(2,1)}) %all-gather.2.cloned.1.call-update) | async-done | bytes 6553616 | tf_op jit(solution)/shard_map/all_gather | solution.py:55
  63.0 6.3 %rev.6 = bf16[8,640,640]{2,1,0:T(8,128)(2,1)} reverse(bf16[8,640,640]{2,1,0:T(8,128)(2,1)} %all-gather.2.cloned.1.call-done), dimensions={0} | reverse | bytes 13107200 | tf_op jit(solution)/shard_map/rev | solution.py:56
  69.3 12.4 %pad_maximum_fusion = bf16[16,640,640]{2,1,0:T(8,128)(2,1)} fusion(bf16[8,640,640]{2,1,0:T(8,128)(2,1)} %all-gather.2.cloned.1.call-done, bf16[8,640,640]{2,1,0:T(8,128)(2,1)} %rev.6), kind=kLoop, calls=%fused_computation.21 | loop fusion | flops 6553600 | bytes 26214400 | tf_op jit(solution)/shard_map/concatenate | solution.py:56
  81.6 36.4 %while.35 = (s32[]{:T(128)}, f32[8,80,640]{2,1,0:T(8,128)}, f32[8,80,640]{2,1,0:T(8,128)}, bf16[8,80,640]{2,1,0:T(8,128)(2,1)}, bf16[16,640,640]{2,1,0:T(8,128)(...) while((s32[]{:T(128)}, f32[8,80,640]{2,1,0:T(8,128)}, ...), condition=%wide.region_1.2_spmd.clone.clone, body=%wide.region_0.1_spmd.clone.clone.sunk | while | flops 592742400 | bytes 19661552 | solution.py:79
  81.6 1.0 dynamic-slice_bitcast_fusion.3
  82.6 4.6 %fusion.48 = f32[9,80,640]{2,1,0:T(8,128)S(1)} fusion(bf16[16,640,640]{2,1,0:T(8,128)(2,1)} %get-tuple-element.458, s32[]{:T(128)} %get-tuple-element.444, pred[9]{0:T(512)(128)(4,1)S(1)} %iota_compare_fusion.7, bf16[80,640]{1,0:T(8,128)(2,1)S(1)} %get-tuple-element.428, bf16[80,640]{1,0:T(8,128)(2,1)S(1)} %get-tuple-element.429), kind=kOutput, calls=%fused_computation.5.clone.1 | convolution fusion | flops 590284800 | bytes 9421321 | tf_op jit(solution)/shard_map/while/body/eval_jaxpr/uik,ukl->uil/dot_general | solution.py:67
  87.2 2.1 %fusion.49 = (f32[8,80,640]{2,1,0:T(8,128)}, f32[8,80,640]{2,1,0:T(8,128)}) fusion(f32[9,80,640]{2,1,0:T(8,128)S(1)} %fusion.48, f32[8,80,640]{2,1,0:T(8,128)} %get-tuple-element.446, pred[8]{0:T(512)(128)(4,1)S(1)} %get-tuple-element.430, pred[]{:T(512)S(6)} %compare.7, pred[8]{0:T(512)(128)(4,1)S(1)} %get-tuple-element.431, ...), kind=kLoop, calls=%fused_computation.8.clone.1 | loop fusion | flops 2457600 | bytes 9830417 | tf_op jit(solution)/shard_map/while/body/eval_jaxpr/add | solution.py:68
  89.3 1.0 dynamic-slice_bitcast_fusion.3
  90.3 4.6 %fusion.48 = f32[9,80,640]{2,1,0:T(8,128)S(1)} fusion(bf16[16,640,640]{2,1,0:T(8,128)(2,1)} %get-tuple-element.458, s32[]{:T(128)} %get-tuple-element.444, pred[9]{0:T(512)(128)(4,1)S(1)} %iota_compare_fusion.7, bf16[80,640]{1,0:T(8,128)(2,1)S(1)} %get-tuple-element.428, bf16[80,640]{1,0:T(8,128)(2,1)S(1)} %get-tuple-element.429), kind=kOutput, calls=%fused_computation.5.clone.1 | convolution fusion | flops 590284800 | bytes 9421321 | tf_op jit(solution)/shard_map/while/body/eval_jaxpr/uik,ukl->uil/dot_general | solution.py:67
  94.9 4.0 %fusion.49 = (f32[8,80,640]{2,1,0:T(8,128)}, f32[8,80,640]{2,1,0:T(8,128)}) fusion(f32[9,80,640]{2,1,0:T(8,128)S(1)} %fusion.48, f32[8,80,640]{2,1,0:T(8,128)} %get-tuple-element.446, pred[8]{0:T(512)(128)(4,1)S(1)} %get-tuple-element.430, pred[]{:T(512)S(6)} %compare.7, pred[8]{0:T(512)(128)(4,1)S(1)} %get-tuple-element.431, ...), kind=kLoop, calls=%fused_computation.8.clone.1 | loop fusion | flops 2457600 | bytes 9830417 | tf_op jit(solution)/shard_map/while/body/eval_jaxpr/add | solution.py:68
  98.9 1.0 dynamic-slice_bitcast_fusion.3
  99.9 4.6 %fusion.48 = f32[9,80,640]{2,1,0:T(8,128)S(1)} fusion(bf16[16,640,640]{2,1,0:T(8,128)(2,1)} %get-tuple-element.458, s32[]{:T(128)} %get-tuple-element.444, pred[9]{0:T(512)(128)(4,1)S(1)} %iota_compare_fusion.7, bf16[80,640]{1,0:T(8,128)(2,1)S(1)} %get-tuple-element.428, bf16[80,640]{1,0:T(8,128)(2,1)S(1)} %get-tuple-element.429), kind=kOutput, calls=%fused_computation.5.clone.1 | convolution fusion | flops 590284800 | bytes 9421321 | tf_op jit(solution)/shard_map/while/body/eval_jaxpr/uik,ukl->uil/dot_general | solution.py:67
  104.5 4.0 %fusion.49 = (f32[8,80,640]{2,1,0:T(8,128)}, f32[8,80,640]{2,1,0:T(8,128)}) fusion(f32[9,80,640]{2,1,0:T(8,128)S(1)} %fusion.48, f32[8,80,640]{2,1,0:T(8,128)} %get-tuple-element.446, pred[8]{0:T(512)(128)(4,1)S(1)} %get-tuple-element.430, pred[]{:T(512)S(6)} %compare.7, pred[8]{0:T(512)(128)(4,1)S(1)} %get-tuple-element.431, ...), kind=kLoop, calls=%fused_computation.8.clone.1 | loop fusion | flops 2457600 | bytes 9830417 | tf_op jit(solution)/shard_map/while/body/eval_jaxpr/add | solution.py:68
  108.5 1.0 dynamic-slice_bitcast_fusion.3
  109.5 4.6 %fusion.48 = f32[9,80,640]{2,1,0:T(8,128)S(1)} fusion(bf16[16,640,640]{2,1,0:T(8,128)(2,1)} %get-tuple-element.458, s32[]{:T(128)} %get-tuple-element.444, pred[9]{0:T(512)(128)(4,1)S(1)} %iota_compare_fusion.7, bf16[80,640]{1,0:T(8,128)(2,1)S(1)} %get-tuple-element.428, bf16[80,640]{1,0:T(8,128)(2,1)S(1)} %get-tuple-element.429), kind=kOutput, calls=%fused_computation.5.clone.1 | convolution fusion | flops 590284800 | bytes 9421321 | tf_op jit(solution)/shard_map/while/body/eval_jaxpr/uik,ukl->uil/dot_general | solution.py:67
  114.1 4.0 %fusion.49 = (f32[8,80,640]{2,1,0:T(8,128)}, f32[8,80,640]{2,1,0:T(8,128)}) fusion(f32[9,80,640]{2,1,0:T(8,128)S(1)} %fusion.48, f32[8,80,640]{2,1,0:T(8,128)} %get-tuple-element.446, pred[8]{0:T(512)(128)(4,1)S(1)} %get-tuple-element.430, pred[]{:T(512)S(6)} %compare.7, pred[8]{0:T(512)(128)(4,1)S(1)} %get-tuple-element.431, ...), kind=kLoop, calls=%fused_computation.8.clone.1 | loop fusion | flops 2457600 | bytes 9830417 | tf_op jit(solution)/shard_map/while/body/eval_jaxpr/add | solution.py:68
  118.1 3.3 %add_multiply_fusion = f32[8,80,640]{2,1,0:T(8,128)} fusion(f32[8,80,640]{2,1,0:T(8,128)} %get-tuple-element.265, f32[8,80,640]{2,1,0:T(8,128)} %get-tuple-element.266), kind=kLoop, calls=%fused_computation.27 | loop fusion | flops 819200 | bytes 4915200 | tf_op jit(solution)/shard_map/mul | solution.py:80
  121.4 0.1 broadcast_in_dim.232
  121.5 8.4 %while.34 = (s32[]{:T(128)}, f32[80,640]{1,0:T(8,128)S(1)}, f32[8,80,640]{2,1,0:T(8,128)S(1)}, f32[80]{0:T(128)S(1)}, f32[8,80,640]{2,1,0:T(8,128)}, /*index=5*/s32[]{:T(128)}, s32[]{:T(128)}) while((s32[]{:T(128)}, f32[80,640]{1,0:T(8,128)S(1)}, f32[8,80,640]{2,1,0:T(8,128)S(1)}, f32[80]{0:T(128)S(1)}, f32[8,80,640]{2,1,0:T(8,128)}, ...), condition=%wide.region_3.4_spmd.clone, body=%wide.region_2.3_spmd.clone.sunk | while | flops 153603 | bytes 819803 | solution.py:89
  121.5 1.0 bitcast_dynamic-update-slice_fusion.2
  122.5 1.0 bitcast_dynamic-update-slice_fusion.2
  123.6 1.0 bitcast_dynamic-update-slice_fusion.2
  124.6 1.0 bitcast_dynamic-update-slice_fusion.2
  125.7 1.0 bitcast_dynamic-update-slice_fusion.2
  126.7 1.0 bitcast_dynamic-update-slice_fusion.2
  127.8 1.0 bitcast_dynamic-update-slice_fusion.2
  128.8 1.0 bitcast_dynamic-update-slice_fusion.2
  129.9 0.3 subtract_convert_fusion
  130.2 19.1 %all_to_all.14 = bf16[8,80,640]{2,1,0:T(8,128)(2,1)S(1)} all-to-all(bf16[8,80,640]{2,1,0:T(8,128)(2,1)S(1)} %subtract_convert_fusion), channel_id=1, replica_groups=mesh['tm'=8,'sector'=4] {'tm'}, dimensions={0} | all-to-all | bytes 1638400 | tf_op jit(solution)/shard_map/all_to_all | solution.py:103
  149.3 0.9 copy.37
  (25 shorter events, 0.3 us)
Async XLA Ops:
  6.5 4.5 %copy-start = (bf16[1,640,640]{2,1,0:T(8,128)(2,1)S(1)}, bf16[1,640,640]{2,1,0:T(8,128)(2,1)}, u32[]{:S(2)}) copy-start(bf16[1,640,640]{2,1,0:T(8,128)(2,1)} %param.11) | copy-start | bytes 2457604
  6.5 4.5 %copy-start.1 = (bf16[1,1,640,640]{3,2,1,0:T(8,128)(2,1)S(1)}, bf16[1,1,640,640]{3,2,1,0:T(8,128)(2,1)}, u32[]{:S(2)}) copy-start(bf16[1,1,640,640]{3,2,1,0:T(8,128)(2,1)} %param.10) | copy-start | bytes 2457604
  6.5 56.4 %all-gather.2.cloned.1.call-start = ((), (), s32[]{:S(2)}) async-start(), calls=%async_computation.2 | async-start | bytes 7372800 | tf_op jit(solution)/shard_map/all_gather | solution.py:55
  9.7 23.4 %collective-permute-start.1 = (bf16[1,640,640]{2,1,0:T(8,128)(2,1)}, bf16[1,640,640]{2,1,0:T(8,128)(2,1)S(1)}, u32[]{:S(2)}, u32[]{:S(2)}) collective-permute-start(bf16[1,640,640]{2,1,0:T(8,128)(2,1)} %and_select_fusion.1), channel_id=1, source_target_pairs={{1,0},{2,1},{3,2},{5,4},{6,5},{7,6},{9,8},{10,9},{11,10},{13,12},{... | collective-permute-start | bytes 2457608 | tf_op jit(solution)/shard_map/ppermute | solution.py:22
  13.9 23.4 %collective-permute-start = (bf16[1,640,640]{2,1,0:T(8,128)(2,1)}, bf16[1,640,640]{2,1,0:T(8,128)(2,1)S(1)}, u32[]{:S(2)}, u32[]{:S(2)}) collective-permute-start(bf16[1,640,640]{2,1,0:T(8,128)(2,1)} %fusion.15), channel_id=1, source_target_pairs={{0,1},{1,2},{2,3},{4,5},{5,6},{6,7},{8,9},{9,10},{10,11},{12,13},{... | collective-permute-start | bytes 2457608 | tf_op jit(solution)/shard_map/ppermute | solution.py:22
  37.3 0.9 copy-start.2
  46.9 34.8 %all-to-all-start = ((bf16[8,1,80,640]{3,2,1,0:T(8,128)(2,1)}), bf16[8,1,80,640]{3,2,1,0:T(8,128)(2,1)}, u32[]{:S(2)}, u32[]{:S(2)}) async-start(bf16[8,1,80,640]{3,2,1,0:T(8,128)(2,1)} %fusion.32), calls=%async_computation | async-start | bytes 1638400 | tf_op jit(solution)/shard_map/all_to_all | solution.py:9
Sparse Core Ops, SparseCore 0:
  9.8 53.0 all-gather.1
